TPU v7x, 32 devices: a whole 2x2x4 slice. The times are simulated.
32 devices in a mesh: dp: 8 (over z, x), tensor: 4 (over y, core).
Axes of the slice: x: 2, y: 2, z: 4, core: 2. Of those that a mesh axis runs over, the one named last changes fastest.
Arguments:
- queries: bfloat16 [8192, 1024], P('dp', 'tensor')
- keys: bfloat16 [8192, 1024], P('dp', 'tensor')
- values: bfloat16 [8192, 1024], P('dp', 'tensor'), may hold values from -6 to 6
- mem_keys: bfloat16 [16384, 1024], P('dp', 'tensor')
- mem_values: bfloat16 [16384, 1024], P('dp', 'tensor'), may hold values from -6 to 6
- gate_bias: float32 [8], P('tensor'), may hold values from -3 to 3
- out_weight: bfloat16 [1024, 7168], P('tensor'), may hold values from -0.25 to 0.25
- retrieved: int32 [64, 4], P('dp'), may hold values from 0 to 127, as said below
- block_slot: int32 [128], replicated, may hold values from 0 to 127, as said below
Outputs:
- mixed: bfloat16 [7168, 8192], P('tensor', 'dp')
Inputs may be any that keep to these rules, and one draw needn't show every extreme that they name: Row b lists the 4 memory blocks retrieved for query block b, all different. Among the 32 entries of the rows of one device, at most 8 name blocks whose slots lie on one device (slot // 16), and these name at most 4 different blocks. `block_slot`: each slot once.
All inputs are finite; a program needn't handle non-finite values.
Results may differ from a plain program's by a relative error of at most 0.014.
Values may be sent and summed in bfloat16 or wider, within the bound.
A program may use at most 128 MiB of HBM per device.

v0:
```python
import jax
import jax.numpy as jnp
from jax import lax
from jax.sharding import PartitionSpec as P

BLOCK = 128
SEG = 512
TOPK = 4
REQ_CAP = 8


def shards(
    queries, keys, values, mem_keys, mem_values, gate_bias, out_weight, retrieved, block_slot
):
    tok_rows, width = queries.shape
    heads_dev = gate_bias.shape[0]
    head_size = width // heads_dev
    score_scale = head_size ** (-0.5)
    seg_count = tok_rows // SEG
    block_count = tok_rows // BLOCK
    peer_count = lax.axis_size("dp")
    local_blocks = mem_keys.shape[0] // BLOCK
    wanted = retrieved.reshape(-1)
    request_count = wanted.shape[0]
    table_ids = jnp.arange(block_slot.shape[0], dtype=jnp.int32)
    slot_global = jnp.sum(
        jnp.where(wanted[:, None] == table_ids[None, :], block_slot[None, :], 0), axis=1
    )
    owner_of = slot_global // local_blocks
    slot_of = slot_global % local_blocks
    request_order = jnp.arange(request_count, dtype=jnp.int32)
    earlier = request_order[None, :] < request_order[:, None]
    same_owner = owner_of[:, None] == owner_of[None, :]
    capacity = REQ_CAP
    position = jnp.sum(same_owner & earlier, axis=1)
    slot_match = (
        owner_of[:, None, None] == jnp.arange(peer_count, dtype=jnp.int32)[None, :, None]
    ) & (position[:, None, None] == jnp.arange(capacity, dtype=jnp.int32)[None, None, :])
    request = jnp.max(jnp.where(slot_match, slot_of[:, None, None], 0), axis=0)
    key_blocks = mem_keys.reshape(local_blocks, BLOCK, width)
    value_blocks = mem_values.reshape(local_blocks, BLOCK, width)
    asked_slots = lax.all_to_all(request, "dp", split_axis=0, concat_axis=0, tiled=True)
    fetched_keys = lax.all_to_all(
        key_blocks[asked_slots], "dp", split_axis=0, concat_axis=0, tiled=True
    )
    fetched_values = lax.all_to_all(
        value_blocks[asked_slots], "dp", split_axis=0, concat_axis=0, tiled=True
    )
    flat_index = owner_of * capacity + position
    chosen_keys = fetched_keys.reshape(peer_count * capacity, BLOCK, width)[flat_index]
    chosen_keys = chosen_keys.reshape(block_count, TOPK * BLOCK, heads_dev, head_size)
    chosen_values = fetched_values.reshape(peer_count * capacity, BLOCK, width)[flat_index]
    chosen_values = chosen_values.reshape(block_count, TOPK * BLOCK, heads_dev, head_size)
    seg_shape = (seg_count, SEG, heads_dev, head_size)
    seg_queries = queries.reshape(seg_shape)
    local_scores = (
        jnp.einsum(
            "sqhd,skhd->shqk",
            seg_queries,
            keys.reshape(seg_shape),
            preferred_element_type=jnp.float32,
        )
        * score_scale
    )
    causal_mask = jnp.arange(SEG)[:, None] >= jnp.arange(SEG)[None, :]
    local_scores = jnp.where(causal_mask[None, None, :, :], local_scores, -jnp.inf)
    local_weights = jax.nn.softmax(local_scores, axis=-1).astype(jnp.bfloat16)
    local_out = jnp.einsum(
        "shqk,skhd->sqhd",
        local_weights,
        values.reshape(seg_shape),
        preferred_element_type=jnp.float32,
    )
    local_out = local_out.reshape(tok_rows, heads_dev, head_size)
    query_blocks = queries.reshape(block_count, BLOCK, heads_dev, head_size)
    mem_scores = (
        jnp.einsum("bqhd,bkhd->bhqk", query_blocks, chosen_keys, preferred_element_type=jnp.float32)
        * score_scale
    )
    mem_weights = jax.nn.softmax(mem_scores, axis=-1).astype(jnp.bfloat16)
    mem_out = jnp.einsum(
        "bhqk,bkhd->bqhd", mem_weights, chosen_values, preferred_element_type=jnp.float32
    )
    mem_out = mem_out.reshape(tok_rows, heads_dev, head_size)
    mem_gate = jax.nn.sigmoid(gate_bias)[None, :, None]
    attended = (
        (mem_gate * mem_out + (1.0 - mem_gate) * local_out)
        .astype(jnp.bfloat16)
        .reshape(tok_rows, width)
    )
    return lax.psum_scatter(
        lax.dot_general(
            out_weight, attended, (((0,), (1,)), ((), ())), preferred_element_type=jnp.float32
        ).astype(jnp.bfloat16),
        "tensor",
        scatter_dimension=0,
        tiled=True,
    )


def solution(mesh):
    in_specs = (
        P("dp", "tensor"),
        P("dp", "tensor"),
        P("dp", "tensor"),
        P("dp", "tensor"),
        P("dp", "tensor"),
        P("tensor"),
        P("tensor", None),
        P("dp", None),
        P(),
    )
    out_specs = P("tensor", "dp")
    return jax.shard_map(shards, mesh=mesh, in_specs=in_specs, out_specs=out_specs, check_vma=False)
```

profile of v0, /device:TPU:17, one launch (start us, length us, event | category | flops | bytes accessed | tf_op | source)
XLA Modules:
  0.0 363.8 jit_solution(15761556125131579949)
XLA Ops:
  6.5 0.0 copy-start
  6.5 0.8 copy.62
  7.4 0.1 eq.66
  7.5 0.8 select_reduce_fusion.1
  8.3 0.2 convert_reduce_fusion
  8.5 0.2 select_reduce_fusion
  8.7 8.6 %all_to_all.22 = s32[8,1,8]{2,1,0:T(1,128)S(1)} all-to-all(s32[8,1,8]{2,1,0:T(1,128)S(1)} %bitcast.82), channel_id=1, replica_groups=mesh['dp'=8,'tensor'=4] {'dp'}, dimensions={0} | all-to-all | bytes 512 | tf_op jit(solution)/shard_map/all_to_all | solution.py:42
  17.4 0.1 reshape.268
  17.4 0.0 copy-done
  17.4 2.8 gather_fusion.2
  20.2 6.7 %all-to-all-start.2 = ((bf16[8,8,128,256]{3,2,1,0:T(8,128)(2,1)}), bf16[8,8,128,256]{3,2,1,0:T(8,128)(2,1)}, u32[]{:S(2)}, u32[]{:S(2)}) async-start(bf16[8,8,128,256]{3,2,1,0:T(8,128)(2,1)} %bitcast.76), calls=%async_computation.2 | async-start | bytes 8388608 | tf_op jit(solution)/shard_map/all_to_all | solution.py:43
  27.0 0.0 copy-done.2
  27.0 2.7 gather_fusion
  29.7 85.4 %all-to-all-done.2 = bf16[8,8,128,256]{3,2,1,0:T(8,128)(2,1)} async-done(((bf16[8,8,128,256]{3,2,1,0:T(8,128)(2,1)}), bf16[8,8,128,256]{3,2,1,0:T(8,128)(2,1)}, u32[]{:S(2)}, u32[]{:S(2)}) %all-to-all-start.2) | async-done | bytes 4194336 | tf_op jit(solution)/shard_map/all_to_all | solution.py:43
  115.1 9.1 %all-to-all-start.1 = ((bf16[8,8,128,256]{3,2,1,0:T(8,128)(2,1)}), bf16[8,8,128,256]{3,2,1,0:T(8,128)(2,1)}, u32[]{:S(2)}, u32[]{:S(2)}) async-start(bf16[8,8,128,256]{3,2,1,0:T(8,128)(2,1)} %bitcast.75), calls=%async_computation.1 | async-start | bytes 8388608 | tf_op jit(solution)/shard_map/all_to_all | solution.py:46
  124.2 0.0 reduce-scatter.2.cloned.1.call-start
  124.2 0.0 copy-done.4
  124.2 0.1 reshape.262
  124.3 0.9 reshape.260
  125.3 0.0 copy-done.5
  125.3 0.1 reshape.263
  125.4 0.0 copy-done.6
  125.4 0.1 reshape.264
  125.5 0.1 iota_compare_fusion
  125.6 0.7 fusion.25
  126.3 2.2 fusion.44
  128.5 1.0 fusion.17
  129.5 0.0 copy-start.7
  129.5 0.6 copy.84
  130.1 0.2 copy.87
  130.3 0.0 copy-done.7
  130.3 0.1 broadcast_bitcast_fusion
  130.4 4.2 %gather_fusion.3 = bf16[32,128,256]{2,1,0:T(8,128)(2,1)} fusion(bf16[64,128,256]{2,1,0:T(8,128)(2,1)} %bitcast.12, s32[1024]{0:T(1024)S(1)} %pad_clamp_fusion), kind=kCustom, calls=%fused_computation.3 | custom fusion | bytes 4194432 | tf_op jit(solution)/shard_map/gather | solution.py:50
  134.6 2.5 reshape.301
  137.2 1.8 fusion.8
  138.9 2.0 copy-done.3
  140.9 1.1 fusion.43
  142.0 70.9 %all-to-all-done.1 = bf16[8,8,128,256]{3,2,1,0:T(8,128)(2,1)} async-done(((bf16[8,8,128,256]{3,2,1,0:T(8,128)(2,1)}), bf16[8,8,128,256]{3,2,1,0:T(8,128)(2,1)}, u32[]{:S(2)}, u32[]{:S(2)}) %all-to-all-start.1) | async-done | bytes 4194336 | tf_op jit(solution)/shard_map/all_to_all | solution.py:46
  212.8 2.9 gather_fusion.1
  215.7 2.0 reshape.300
  217.8 6.1 %fusion.18 = f32[8,128,2,128]{1,3,2,0:T(8,128)S(1)} fusion(f32[8,2,128]{2,1,0:T(2,128)S(1)} %fusion.43, bf16[8,512,2,128]{3,2,1,0:T(2,128)(2,1)} %reshape.300, f32[8,2,512,128]{3,2,1,0:T(8,128)} %copy-done.3), kind=kOutput, calls=%fused_computation.27 | convolution fusion | flops 273680896 | bytes 7348224 | tf_op jit(solution)/shard_map/bhqk,bkhd->bqhd/dot_general | solution.py:81
  223.8 0.6 copy.70
  224.4 9.7 %convert_bitcast_fusion = bf16[7168,1024]{0,1:T(8,128)(2,1)} fusion(bf16[256,7168]{1,0:T(8,128)(2,1)} %param.15, f32[32,8,8,128]{3,2,1,0:T(8,128)S(1)} %bitcast.79, f32[1024,256]{0,1:T(8,128)S(1)} %bitcast.78, f32[256]{0:T(256)S(1)} %get-tuple-element.13, f32[256]{0:T(256)S(1)} %get-tuple-element.14), kind=kOutput, calls=%fused_computation.6 | convolution fusion | flops 3766484992 | bytes 20449280 | tf_op jit(solution)/shard_map/dot_general | solution.py:92
  234.2 0.0 reduce-scatter.2.cloned.1.call-update
  234.2 0.0 copy-start.1
  234.2 116.8 %reduce-scatter.2.cloned.1.call-done = bf16[1792,1024]{0,1:T(8,128)(2,1)} async-done(((bf16[7168,1024]{0,1:T(8,128)(2,1)}), bf16[1792,1024]{0,1:T(8,128)(2,1)}) %reduce-scatter.2.cloned.1.call-update) | async-done | bytes 3670032 | tf_op jit(solution)/shard_map/reduce_scatter | solution.py:91
  351.0 5.9 %copy.77 = bf16[1792,1024]{1,0:T(8,128)(2,1)} copy(bf16[1792,1024]{0,1:T(8,128)(2,1)} %reduce-scatter.2.cloned.1.call-done) | data formatting | bytes 7340032 | tf_op jit(solution)/shard_map/reduce_scatter | solution.py:91
  357.0 0.0 copy-done.1
  (12 shorter events, 0.1 us)
Async XLA Ops:
  6.5 10.9 %copy-start = (bf16[2048,256]{1,0:T(8,128)(2,1)S(1)}, bf16[2048,256]{1,0:T(8,128)(2,1)}, u32[]{:S(2)}) copy-start(bf16[2048,256]{1,0:T(8,128)(2,1)} %param.12) | copy-start | bytes 3145732
  20.2 6.7 %copy-start.2 = (bf16[2048,256]{1,0:T(8,128)(2,1)S(1)}, bf16[2048,256]{1,0:T(8,128)(2,1)}, u32[]{:S(2)}) copy-start(bf16[2048,256]{1,0:T(8,128)(2,1)} %param.13) | copy-start | bytes 3145732
  20.2 94.9 %all-to-all-start.2 = ((bf16[8,8,128,256]{3,2,1,0:T(8,128)(2,1)}), bf16[8,8,128,256]{3,2,1,0:T(8,128)(2,1)}, u32[]{:S(2)}, u32[]{:S(2)}) async-start(bf16[8,8,128,256]{3,2,1,0:T(8,128)(2,1)} %bitcast.76), calls=%async_computation.2 | async-start | bytes 8388608 | tf_op jit(solution)/shard_map/all_to_all | solution.py:43
  115.1 9.1 %copy-start.4 = (bf16[1024,256]{1,0:T(8,128)(2,1)S(1)}, bf16[1024,256]{1,0:T(8,128)(2,1)}, u32[]{:S(2)}) copy-start(bf16[1024,256]{1,0:T(8,128)(2,1)} %param.9) | copy-start | bytes 1572868
  115.1 10.2 %copy-start.5 = (bf16[1024,256]{1,0:T(8,128)(2,1)S(1)}, bf16[1024,256]{1,0:T(8,128)(2,1)}, u32[]{:S(2)}) copy-start(bf16[1024,256]{1,0:T(8,128)(2,1)} %param.10) | copy-start | bytes 1572868
  115.1 10.3 %copy-start.6 = (bf16[1024,256]{1,0:T(8,128)(2,1)S(1)}, bf16[1024,256]{1,0:T(8,128)(2,1)}, u32[]{:S(2)}) copy-start(bf16[1024,256]{1,0:T(8,128)(2,1)} %param.11) | copy-start | bytes 1572868
  115.1 97.7 %all-to-all-start.1 = ((bf16[8,8,128,256]{3,2,1,0:T(8,128)(2,1)}), bf16[8,8,128,256]{3,2,1,0:T(8,128)(2,1)}, u32[]{:S(2)}, u32[]{:S(2)}) async-start(bf16[8,8,128,256]{3,2,1,0:T(8,128)(2,1)} %bitcast.75), calls=%async_computation.1 | async-start | bytes 8388608 | tf_op jit(solution)/shard_map/all_to_all | solution.py:46
  124.2 226.9 %reduce-scatter.2.cloned.1.call-start = ((), (), s32[]{:S(2)}) async-start(), calls=%async_computation.4 | async-start | bytes 18350080 | tf_op jit(solution)/shard_map/reduce_scatter | solution.py:91
  129.5 0.8 copy-start.7
  138.9 2.0 copy-start.3
  234.2 122.8 %copy-start.1 = (bf16[2048,256]{1,0:T(8,128)(2,1)S(1)}, bf16[2048,256]{1,0:T(8,128)(2,1)}, u32[]{:S(2)}) copy-start(bf16[2048,256]{1,0:T(8,128)(2,1)} %param.12) | copy-start | bytes 3145732
Sparse Core Ops, SparseCore 0:
  234.3 116.6 reduce-scatter.1
where the time goes:
time: 366 us; the launch traced here: 364 us
  waiting for transfers between devices  273 us (75%)
  local copies, waits for them, and re-layouts  28.9 us (8%)
  matrix products  19.2 us (5%)
  starting transfers between devices  15.8 us (4%)
  between operations  13.6 us (4%)
  blocking collectives  8.61 us (2%)
  other arithmetic  4.6 us (1%)
    reduce_scatter x1, waiting for transfers between devices, shards(): lax.psum_scatter(lax.dot_general(out_weight, attended, (((0,), (1,)), (()...  117 us
    all_to_all x1, waiting for transfers between devices, shards(): lax.all_to_all(key_blocks[asked_slots], 'dp', split_axis=0, concat_axis=0...  85.4 us
    all_to_all x1, waiting for transfers between devices, shards(): lax.all_to_all(value_blocks[asked_slots], 'dp', split_axis=0, concat_axis...  70.9 us
    dot_general x1, matrix products, shards(): lax.dot_general(out_weight, attended, (((0,), (1,)), ((), ())), preferred...  9.71 us
    all_to_all x1, starting transfers between devices, shards(): lax.all_to_all(value_blocks[asked_slots], 'dp', split_axis=0, concat_axis...  9.06 us
    all_to_all x1, blocking collectives, shards(): lax.all_to_all(request, 'dp', split_axis=0, concat_axis=0, tiled=True)  8.61 us
  transfers between devices with their start and end apart: 3, of which 3 were waited for; matrix products, arithmetic and copies ran while one was open for 5% of the time, Pallas kernels for 0%

commit v1 on v0

v1 whole, which is shorter than its diff:
```python
import functools
import math

import jax
import jax.numpy as jnp
from jax import lax
from jax.experimental import pallas as pl
from jax.experimental.pallas import tpu as pltpu
from jax.sharding import PartitionSpec as P

BLOCK = 128
SEG = 512
TOPK = 4
UNIQ_CAP = 4
MESH = pl.DeviceIdType.MESH
NT = (((1,), (1,)), ((), ()))


def flipped(index, mask):
    bit = 1
    result = index
    while bit <= mask:
        if mask & bit:
            result = result + bit * (1 - 2 * (lax.rem(lax.div(index, bit), 2)))
        bit *= 2
    return result


def layer_kernel(
    peers, groups, heads, sliced,
    place_ref, req_ref, gate_ref, q_hbm, k_hbm, v_hbm, mk_hbm, mv_hbm, w_hbm,
    ag_hbm, wg_hbm,
    q_vm, k_vm, v_vm, mk_vm, mv_vm, req_in, req_sm, send_k, send_v, recv_k, recv_v,
    probs, coef, local, att,
    in_sem, smem_sem, own_sem, req_ss, req_rs, k_ss, k_rs, v_ss, v_rs, w_ss, w_rs,
    a_ss, a_rs, f_ss, f_rs,
):
    me = lax.axis_index("dp")
    tme = lax.axis_index("tensor")
    tok, width = q_vm.shape
    head = width // heads
    feats = wg_hbm.shape[1]
    scale = head ** -0.5 * math.log2(math.e)
    chunks = a_ss.shape[0]
    crow = tok // chunks

    loads = [
        pltpu.make_async_copy(src, dst, in_sem.at[i])
        for i, (src, dst) in enumerate(
            ((mk_hbm, mk_vm), (mv_hbm, mv_vm), (q_hbm, q_vm), (k_hbm, k_vm), (v_hbm, v_vm))
        )
    ]
    for load in loads:
        load.start()

    barrier = pltpu.get_barrier_semaphore()
    for m in range(1, peers):
        pl.semaphore_signal(barrier, inc=1, device_id={"dp": flipped(me, m)}, device_id_type=MESH)
    for m in range(1, groups):
        pl.semaphore_signal(
            barrier, inc=1, device_id={"tensor": flipped(tme, m)}, device_id_type=MESH
        )
    pl.semaphore_wait(barrier, peers - 1 + groups - 1)

    order = list(range(peers // 2, peers)) + list(range(peers // 2 - 1, 0, -1))

    req_copies = []
    for m in order:
        peer = flipped(me, m)
        copy = pltpu.make_async_remote_copy(
            src_ref=req_ref.at[peer], dst_ref=req_in.at[m], send_sem=req_ss.at[m],
            recv_sem=req_rs.at[m], device_id={"dp": peer}, device_id_type=MESH,
        )
        copy.start()
        req_copies.append(copy)

    def weight_part(t):
        if sliced:
            return w_hbm.at[:, pl.ds(pl.multiple_of(t * feats, 128), feats)]
        return w_hbm.at[t]

    def weight_place(t):
        return wg_hbm.at[pl.ds(pl.multiple_of(t * width, 128), width)]

    w_copies = []
    for m in range(1, groups):
        peer = flipped(tme, m)
        copy = pltpu.make_async_remote_copy(
            src_ref=weight_part(peer), dst_ref=weight_place(tme), send_sem=w_ss.at[m],
            recv_sem=w_rs.at[m], device_id={"tensor": peer}, device_id_type=MESH,
        )
        copy.start()
        w_copies.append(copy)
    own_w = pltpu.make_async_copy(weight_part(tme), weight_place(tme), own_sem.at[0])
    own_w.start()

    own_req = pltpu.make_async_copy(req_ref.at[me], req_in.at[0], own_sem.at[1])
    own_req.start()
    own_req.wait()
    for copy in req_copies:
        copy.wait()
    to_smem = pltpu.make_async_copy(req_in, req_sm, smem_sem)
    to_smem.start()
    loads[0].wait()
    to_smem.wait()

    def ship(source, send, recv, ss, rs):
        copies = []
        for m in order:
            peer = flipped(me, m)
            for c in range(UNIQ_CAP):
                send[m, c] = source[req_sm[m, 0, c]]
            copy = pltpu.make_async_remote_copy(
                src_ref=send.at[m], dst_ref=recv.at[me], send_sem=ss.at[m],
                recv_sem=rs.at[m], device_id={"dp": peer}, device_id_type=MESH,
            )
            copy.start()
            copies.append(copy)
        for c in range(UNIQ_CAP):
            recv[me, c] = source[req_sm[0, 0, c]]
        return copies

    k_copies = ship(mk_vm, send_k, recv_k, k_ss, k_rs)
    loads[1].wait()
    v_copies = ship(mv_vm, send_v, recv_v, v_ss, v_rs)
    for load in loads[2:]:
        load.wait()

    blocks_seg = SEG // BLOCK

    def local_segment(s, carry):
        base = pl.multiple_of(s * SEG, SEG)
        for h in range(heads):
            cols = slice(h * head, (h + 1) * head)
            gate = gate_ref[:, cols]
            for i in range(blocks_seg):
                span = (i + 1) * BLOCK
                rows = pl.ds(pl.multiple_of(base + i * BLOCK, BLOCK), BLOCK)
                scores = lax.dot_general(
                    q_vm[rows, cols], k_vm[pl.ds(base, span), cols], NT,
                    preferred_element_type=jnp.float32,
                )
                row = lax.broadcasted_iota(jnp.int32, (BLOCK, span), 0) + i * BLOCK
                col = lax.broadcasted_iota(jnp.int32, (BLOCK, span), 1)
                scores = jnp.where(col <= row, scores, -jnp.inf)
                top = jnp.max(scores, axis=1, keepdims=True)
                weights = jnp.exp2((scores - top) * scale)
                total = jnp.sum(weights, axis=1, keepdims=True)
                out = jnp.dot(
                    weights.astype(jnp.bfloat16), v_vm[pl.ds(base, span), cols],
                    preferred_element_type=jnp.float32,
                )
                local[rows, cols] = out * ((1.0 - gate) / total)
        return carry

    lax.fori_loop(0, tok // SEG, local_segment, 0)

    for copy in k_copies:
        copy.wait_recv()

    def mem_scores(b, carry):
        rows = pl.ds(pl.multiple_of(b * BLOCK, BLOCK), BLOCK)
        found = [
            recv_k[place_ref[0, b * TOPK + j], place_ref[1, b * TOPK + j]] for j in range(TOPK)
        ]
        for h in range(heads):
            cols = slice(h * head, (h + 1) * head)
            keys = jnp.concatenate([block[:, cols] for block in found], axis=0)
            scores = lax.dot_general(
                q_vm[rows, cols], keys, NT, preferred_element_type=jnp.float32
            )
            top = jnp.max(scores, axis=1, keepdims=True)
            weights = jnp.exp2((scores - top) * scale)
            total = jnp.sum(weights, axis=1, keepdims=True)
            probs[b, h] = weights.astype(jnp.bfloat16)
            coef[rows, cols] = gate_ref[:, cols] / total
        return carry

    lax.fori_loop(0, tok // BLOCK, mem_scores, 0)

    for copy in v_copies:
        copy.wait_recv()

    def mem_values(b, carry):
        rows = pl.ds(pl.multiple_of(b * BLOCK, BLOCK), BLOCK)
        found = [
            recv_v[place_ref[0, b * TOPK + j], place_ref[1, b * TOPK + j]] for j in range(TOPK)
        ]
        for h in range(heads):
            cols = slice(h * head, (h + 1) * head)
            vals = jnp.concatenate([block[:, cols] for block in found], axis=0)
            out = jnp.dot(probs[b, h], vals, preferred_element_type=jnp.float32)
            att[rows, cols] = (coef[rows, cols] * out + local[rows, cols]).astype(att.dtype)
        return carry

    def att_place(t, c):
        return ag_hbm.at[
            pl.ds(c * crow, crow), pl.ds(pl.multiple_of(t * width, 128), width)
        ]

    mate = flipped(tme, 1)
    others = list(range(2, groups, 2))
    a_copies = {}
    own_copies = [own_w]
    for c in range(chunks):
        lax.fori_loop(c * crow // BLOCK, (c + 1) * crow // BLOCK, mem_values, 0)
        mine = att.at[pl.ds(c * crow, crow)]
        for m in others + [1]:
            copy = pltpu.make_async_remote_copy(
                src_ref=mine, dst_ref=att_place(tme, c), send_sem=a_ss.at[c, m],
                recv_sem=a_rs.at[c, m], device_id={"tensor": flipped(tme, m)},
                device_id_type=MESH,
            )
            copy.start()
            a_copies[c, m] = copy
        own = pltpu.make_async_copy(mine, att_place(tme, c), own_sem.at[2 + c])
        own.start()
        own_copies.append(own)

    f_copies = []
    for c in range(chunks):
        for m in others:
            a_copies[c, m].wait_recv()
            part = att_place(flipped(tme, m), c)
            copy = pltpu.make_async_remote_copy(
                src_ref=part, dst_ref=part, send_sem=f_ss.at[c, m], recv_sem=f_rs.at[c, m],
                device_id={"tensor": mate}, device_id_type=MESH,
            )
            copy.start()
            f_copies.append(copy)
    for c in range(chunks):
        a_copies[c, 1].wait_recv()
    for copy in f_copies:
        copy.wait()
    for copy in a_copies.values():
        copy.wait_send()
    for copy in w_copies:
        copy.wait()
    for copy in k_copies + v_copies:
        copy.wait_send()
    for copy in own_copies:
        copy.wait()


def request_plan(retrieved, block_slot, local_blocks, peer_count):
    wanted = retrieved.reshape(-1)
    count = wanted.shape[0]
    table_ids = jnp.arange(block_slot.shape[0], dtype=jnp.int32)
    slot = jnp.sum(
        jnp.where(wanted[:, None] == table_ids[None, :], block_slot[None, :], 0), axis=1
    )
    owner = slot // local_blocks
    number = jnp.arange(count, dtype=jnp.int32)
    same = slot[:, None] == slot[None, :]
    first = jnp.min(jnp.where(same, number[None, :], count), axis=1)
    leads = first == number
    before = (
        leads[None, :] & (owner[:, None] == owner[None, :]) & (number[None, :] < first[:, None])
    )
    position = jnp.sum(before.astype(jnp.int32), axis=1)
    peer_ids = jnp.arange(peer_count, dtype=jnp.int32)
    lanes = jnp.arange(128, dtype=jnp.int32)
    match = (owner[:, None, None] == peer_ids[None, :, None]) & (
        position[:, None, None] == lanes[None, None, :]
    )
    request = jnp.max(jnp.where(match, (slot % local_blocks)[:, None, None], 0), axis=0)
    return jnp.stack([owner, position]), request


def shards(
    queries, keys, values, mem_keys, mem_values, gate_bias, out_weight, retrieved, block_slot
):
    tok, width = queries.shape
    heads = gate_bias.shape[0]
    head = width // heads
    peers = lax.axis_size("dp")
    groups = lax.axis_size("tensor")
    local_blocks = mem_keys.shape[0] // BLOCK
    feats = out_weight.shape[1] // groups
    chunks = tok // 256
    place, request = request_plan(retrieved, block_slot, local_blocks, peers)
    request = jnp.broadcast_to(request[:, None, :], (peers, 8, 128))
    gate_row = jnp.repeat(jax.nn.sigmoid(gate_bias), head)[None, :]
    sliced = feats % 128 == 0
    weight = out_weight
    if not sliced:
        weight = out_weight.reshape(width, groups, feats).transpose(1, 0, 2)
    blocked = (local_blocks, BLOCK, width)
    bf16 = jnp.bfloat16
    dma = pltpu.SemaphoreType.DMA
    any_spec = pl.BlockSpec(memory_space=pl.ANY)
    gathered, weights = pl.pallas_call(
        functools.partial(layer_kernel, peers, groups, heads, sliced),
        out_shape=(
            jax.ShapeDtypeStruct((tok, groups * width), bf16),
            jax.ShapeDtypeStruct((groups * width, feats), bf16),
        ),
        in_specs=[
            pl.BlockSpec(memory_space=pltpu.SMEM),
            pl.BlockSpec(memory_space=pltpu.VMEM),
            pl.BlockSpec(memory_space=pltpu.VMEM),
        ]
        + [any_spec] * 6,
        out_specs=(any_spec, any_spec),
        scratch_shapes=[
            pltpu.VMEM((tok, width), bf16),
            pltpu.VMEM((tok, width), bf16),
            pltpu.VMEM((tok, width), bf16),
            pltpu.VMEM(blocked, bf16),
            pltpu.VMEM(blocked, bf16),
            pltpu.VMEM((peers, 8, 128), jnp.int32),
            pltpu.SMEM((peers, 8, 128), jnp.int32),
            pltpu.VMEM((peers, UNIQ_CAP, BLOCK, width), bf16),
            pltpu.VMEM((peers, UNIQ_CAP, BLOCK, width), bf16),
            pltpu.VMEM((peers, UNIQ_CAP, BLOCK, width), bf16),
            pltpu.VMEM((peers, UNIQ_CAP, BLOCK, width), bf16),
            pltpu.VMEM((tok // BLOCK, heads, BLOCK, TOPK * BLOCK), bf16),
            pltpu.VMEM((tok, width), jnp.float32),
            pltpu.VMEM((tok, width), jnp.float32),
            pltpu.VMEM((tok, width), bf16),
            dma((5,)),
            dma(()),
            dma((2 + chunks,)),
            dma((peers,)),
            dma((peers,)),
            dma((peers,)),
            dma((peers,)),
            dma((peers,)),
            dma((peers,)),
            dma((groups,)),
            dma((groups,)),
            dma((chunks, groups)),
            dma((chunks, groups)),
            dma((chunks, groups)),
            dma((chunks, groups)),
        ],
        compiler_params=pltpu.CompilerParams(
            collective_id=0, has_side_effects=True, vmem_limit_bytes=52 * 2**20
        ),
        name="memory_layer",
    )(
        place, request, gate_row, queries, keys, values,
        mem_keys.reshape(blocked), mem_values.reshape(blocked), weight,
    )
    return lax.dot_general(
        weights, gathered, (((0,), (1,)), ((), ())), preferred_element_type=jnp.float32
    ).astype(bf16)


def solution(mesh):
    in_specs = (
        P("dp", "tensor"),
        P("dp", "tensor"),
        P("dp", "tensor"),
        P("dp", "tensor"),
        P("dp", "tensor"),
        P("tensor"),
        P("tensor", None),
        P("dp", None),
        P(),
    )
    out_specs = P("tensor", "dp")
    return jax.shard_map(shards, mesh=mesh, in_specs=in_specs, out_specs=out_specs, check_vma=False)
```

time: 366 us -> 133 us (0.36)
  waiting for transfers between devices: 273 us -> 0 us
  Pallas kernels: 0 us -> 118 us
  local copies, waits for them, and re-layouts: 28.9 us -> 4.04 us
  starting transfers between devices: 15.8 us -> 0 us
  between operations: 13.6 us -> 0.06 us
  matrix products: 19.2 us -> 8.58 us
  blocking collectives: 8.61 us -> 0 us
    all_to_all x2 -> x0, waiting for transfers between devices: 156 us -> none  [the longest x1 85.4 us: shards(): lax.all_to_all(key_blocks[asked_slots], 'dp', split_axis=0, concat_axis=0...]
    pallas_call x0 -> x1, Pallas kernels: none -> 118 us  [shards(): pl.pallas_call(functools.partial(layer_kernel, peers, groups, heads, slic...]
    reduce_scatter x1 -> x0, waiting for transfers between devices: 117 us -> none  [shards(): lax.psum_scatter(lax.dot_general(out_weight, attended, (((0,), (1,)), (()...]
    all_to_all x2 -> x0, starting transfers between devices: 15.8 us -> none  [the longest x1 9.06 us: shards(): lax.all_to_all(value_blocks[asked_slots], 'dp', split_axis=0, concat_axis...]
    gather x4 -> x0, local copies, waits for them, and re-layouts: 12.6 us -> none  [the longest x1 4.19 us: shards(): fetched_keys.reshape(peer_count * capacity, BLOCK, width)[flat_index]]
    dot_general x5 -> x1, matrix products: 19.2 us -> 8.58 us  [shards(): lax.dot_general(weights, gathered, (((0,), (1,)), ((), ())), preferred_el...]
    all_to_all x1 -> x0, blocking collectives: 8.61 us -> none  [shards(): lax.all_to_all(request, 'dp', split_axis=0, concat_axis=0, tiled=True)]
    reshape x7 -> x0, local copies, waits for them, and re-layouts: 6.48 us -> none  [the longest x1 2.54 us: shards(): chosen_keys.reshape(block_count, TOPK * BLOCK, heads_dev, head_size)]
  transfers between devices with their start and end apart: 3 -> 0, of which waited for: 3 -> 0; matrix products, arithmetic and copies ran while one was open for 5% -> 0% of each run, Pallas kernels for 0% -> 0%
where the time goes in v1:
time: 133 us
  Pallas kernels  118 us (89%)
  matrix products  8.58 us (6%)
  local copies, waits for them, and re-layouts  4.04 us (3%)
  other arithmetic  2.19 us (2%)
    pallas_call x1, Pallas kernels, shards(): pl.pallas_call(functools.partial(layer_kernel, peers, groups, heads, slic...  118 us
    dot_general x1, matrix products, shards(): lax.dot_general(weights, gathered, (((0,), (1,)), ((), ())), preferred_el...  8.58 us
    unnamed x7, local copies, waits for them, and re-layouts  3.88 us

profile of v1, /device:TPU:17, one launch (start us, length us, event | category | flops | bytes accessed | tf_op | source)
XLA Modules:
  0.0 133.0 jit_solution(14285714154324454374)
XLA Ops:
  0.0 0.7 add_divide_fusion
  0.7 0.1 broadcast_in_dim.70
  0.7 0.8 copy.12
  1.5 0.1 eq.86
  1.6 0.8 select_reduce_fusion.2
  2.4 0.2 select_reduce_fusion.1
  2.7 0.2 convert_reduce_fusion
  2.8 0.1 iota_compare_fusion
  2.9 0.1 iota_compare_fusion.1
  3.0 0.1 select_reduce_fusion
  3.2 0.0 copy-start
  3.2 1.0 copy-done
  4.2 0.0 copy-start.1
  4.2 1.0 copy-done.1
  5.2 0.0 copy-start.2
  5.3 1.0 copy-done.2
  6.3 118.2 %memory_layer.1 = (bf16[1024,1024]{1,0:T(8,128)(2,1)}, bf16[1024,1792]{1,0:T(8,128)(2,1)}) custom-call(s32[2,32]{1,0:T(2,128)S(1)} %pad_add_fusion.place_ref, s32[8,8,128]{2,1,0:T(8,128)S(1)} %broadcast_in_dim.69.req_ref, f32[1,256]{1,0:T(1,128)S(1)} %bitcast.14, bf16[1024,256]{1,0:T(8,128)(2,1)S(1)} %copy-done, bf16[1024,256]{1,0:T(8,128)(2,1)S(1)} %copy-done.1, ...), custom_call_target="tpu_custom_call" | custom-call | tf_op jit(solution)/shard_map/memory_layer/pallas_call | solution.py:292
  124.5 8.6 %convolution_convert_fusion = bf16[1792,1024]{1,0:T(8,128)(2,1)} fusion(bf16[1024,1792]{1,0:T(8,128)(2,1)} %get-tuple-element.7, bf16[1024,1024]{1,0:T(8,128)(2,1)} %get-tuple-element.8), kind=kOutput, calls=%fused_computation | convolution fusion | flops 3759931392 | bytes 9437184 | tf_op jit(solution)/shard_map/dot_general | solution.py:345
  (5 shorter events, 0.0 us)
Async XLA Ops:
  3.2 1.0 copy-start
  4.2 1.0 copy-start.1
  5.2 1.0 copy-start.2

commit v2 on v1

--- a/solution.py
+++ b/solution.py
@@ -41,7 +41,7 @@
     head = width // heads
     feats = wg_hbm.shape[1]
     scale = head ** -0.5 * math.log2(math.e)
-    chunks = a_ss.shape[0]
+    chunks = a_ss.shape[1]
     crow = tok // chunks
 
     loads = [
@@ -104,25 +104,29 @@
     loads[0].wait()
     to_smem.wait()
 
-    def ship(source, send, recv, ss, rs):
+    def ship(source, h, send, recv, ss, rs):
         copies = []
+        cols = slice(h * head, (h + 1) * head)
         for m in order:
             peer = flipped(me, m)
             for c in range(UNIQ_CAP):
-                send[m, c] = source[req_sm[m, 0, c]]
+                send[h, m, c] = source[req_sm[m, 0, c], :, cols]
             copy = pltpu.make_async_remote_copy(
-                src_ref=send.at[m], dst_ref=recv.at[me], send_sem=ss.at[m],
-                recv_sem=rs.at[m], device_id={"dp": peer}, device_id_type=MESH,
+                src_ref=send.at[h, m], dst_ref=recv[h].at[me], send_sem=ss.at[h, m],
+                recv_sem=rs.at[h, m], device_id={"dp": peer}, device_id_type=MESH,
             )
             copy.start()
             copies.append(copy)
         for c in range(UNIQ_CAP):
-            recv[me, c] = source[req_sm[0, 0, c]]
+            recv[h][me, c] = source[req_sm[0, 0, c], :, cols]
         return copies
 
-    k_copies = ship(mk_vm, send_k, recv_k, k_ss, k_rs)
-    loads[1].wait()
-    v_copies = ship(mv_vm, send_v, recv_v, v_ss, v_rs)
+    k_copies, v_copies = [], []
+    for h in range(heads):
+        k_copies.append(ship(mk_vm, h, send_k, recv_k, k_ss, k_rs))
+        if h == 0:
+            loads[1].wait()
+        v_copies.append(ship(mv_vm, h, send_v, recv_v, v_ss, v_rs))
     for load in loads[2:]:
         load.wait()
 
@@ -155,89 +159,96 @@
 
     lax.fori_loop(0, tok // SEG, local_segment, 0)
 
-    for copy in k_copies:
-        copy.wait_recv()
-
-    def mem_scores(b, carry):
+    def fetched(recv, h, b):
+        return jnp.concatenate(
+            [
+                recv[h][place_ref[0, b * TOPK + j], place_ref[1, b * TOPK + j]]
+                for j in range(TOPK)
+            ],
+            axis=0,
+        )
+
+    def mem_scores(h, b, carry):
         rows = pl.ds(pl.multiple_of(b * BLOCK, BLOCK), BLOCK)
-        found = [
-            recv_k[place_ref[0, b * TOPK + j], place_ref[1, b * TOPK + j]] for j in range(TOPK)
-        ]
-        for h in range(heads):
-            cols = slice(h * head, (h + 1) * head)
-            keys = jnp.concatenate([block[:, cols] for block in found], axis=0)
-            scores = lax.dot_general(
-                q_vm[rows, cols], keys, NT, preferred_element_type=jnp.float32
-            )
-            top = jnp.max(scores, axis=1, keepdims=True)
-            weights = jnp.exp2((scores - top) * scale)
-            total = jnp.sum(weights, axis=1, keepdims=True)
-            probs[b, h] = weights.astype(jnp.bfloat16)
-            coef[rows, cols] = gate_ref[:, cols] / total
+        cols = slice(h * head, (h + 1) * head)
+        scores = lax.dot_general(
+            q_vm[rows, cols], fetched(recv_k, h, b), NT, preferred_element_type=jnp.float32
+        )
+        top = jnp.max(scores, axis=1, keepdims=True)
+        weights = jnp.exp2((scores - top) * scale)
+        total = jnp.sum(weights, axis=1, keepdims=True)
+        probs[b] = weights.astype(jnp.bfloat16)
+        coef[rows, :] = gate_ref[:, cols] / total
         return carry
 
-    lax.fori_loop(0, tok // BLOCK, mem_scores, 0)
-
-    for copy in v_copies:
-        copy.wait_recv()
-
-    def mem_values(b, carry):
+    def mem_values(h, b, carry):
         rows = pl.ds(pl.multiple_of(b * BLOCK, BLOCK), BLOCK)
-        found = [
-            recv_v[place_ref[0, b * TOPK + j], place_ref[1, b * TOPK + j]] for j in range(TOPK)
-        ]
-        for h in range(heads):
-            cols = slice(h * head, (h + 1) * head)
-            vals = jnp.concatenate([block[:, cols] for block in found], axis=0)
-            out = jnp.dot(probs[b, h], vals, preferred_element_type=jnp.float32)
-            att[rows, cols] = (coef[rows, cols] * out + local[rows, cols]).astype(att.dtype)
+        cols = slice(h * head, (h + 1) * head)
+        out = jnp.dot(probs[b], fetched(recv_v, h, b), preferred_element_type=jnp.float32)
+        att[h, rows, :] = (coef[rows, :] * out + local[rows, cols]).astype(att.dtype)
         return carry
 
-    def att_place(t, c):
-        return ag_hbm.at[
-            pl.ds(c * crow, crow), pl.ds(pl.multiple_of(t * width, 128), width)
-        ]
+    def att_place(t, h, c):
+        column = pl.multiple_of(t * width + h * head, 128)
+        return ag_hbm.at[pl.ds(c * crow, crow), pl.ds(column, head)]
 
     mate = flipped(tme, 1)
     others = list(range(2, groups, 2))
-    a_copies = {}
+    a_copies, f_copies = {}, []
     own_copies = [own_w]
-    for c in range(chunks):
-        lax.fori_loop(c * crow // BLOCK, (c + 1) * crow // BLOCK, mem_values, 0)
-        mine = att.at[pl.ds(c * crow, crow)]
-        for m in others + [1]:
-            copy = pltpu.make_async_remote_copy(
-                src_ref=mine, dst_ref=att_place(tme, c), send_sem=a_ss.at[c, m],
-                recv_sem=a_rs.at[c, m], device_id={"tensor": flipped(tme, m)},
-                device_id_type=MESH,
+
+    def forward(h):
+        for c in range(chunks):
+            for m in others:
+                a_copies[h, c, m].wait_recv()
+                part = att_place(flipped(tme, m), h, c)
+                copy = pltpu.make_async_remote_copy(
+                    src_ref=part, dst_ref=part, send_sem=f_ss.at[h, c, m],
+                    recv_sem=f_rs.at[h, c, m], device_id={"tensor": mate}, device_id_type=MESH,
+                )
+                copy.start()
+                f_copies.append(copy)
+
+    for h in range(heads):
+        for copy in k_copies[h]:
+            copy.wait_recv()
+        lax.fori_loop(0, tok // BLOCK, functools.partial(mem_scores, h), 0)
+        if h > 0:
+            forward(h - 1)
+        for copy in v_copies[h]:
+            copy.wait_recv()
+        for c in range(chunks):
+            lax.fori_loop(
+                c * crow // BLOCK, (c + 1) * crow // BLOCK, functools.partial(mem_values, h), 0
             )
-            copy.start()
-            a_copies[c, m] = copy
-        own = pltpu.make_async_copy(mine, att_place(tme, c), own_sem.at[2 + c])
-        own.start()
-        own_copies.append(own)
-
-    f_copies = []
-    for c in range(chunks):
-        for m in others:
-            a_copies[c, m].wait_recv()
-            part = att_place(flipped(tme, m), c)
-            copy = pltpu.make_async_remote_copy(
-                src_ref=part, dst_ref=part, send_sem=f_ss.at[c, m], recv_sem=f_rs.at[c, m],
-                device_id={"tensor": mate}, device_id_type=MESH,
+            mine = att.at[h, pl.ds(c * crow, crow)]
+            for m in others + [1]:
+                copy = pltpu.make_async_remote_copy(
+                    src_ref=mine, dst_ref=att_place(tme, h, c), send_sem=a_ss.at[h, c, m],
+                    recv_sem=a_rs.at[h, c, m], device_id={"tensor": flipped(tme, m)},
+                    device_id_type=MESH,
+                )
+                copy.start()
+                a_copies[h, c, m] = copy
+            own = pltpu.make_async_copy(
+                mine, att_place(tme, h, c), own_sem.at[2 + h * chunks + c]
             )
-            copy.start()
-            f_copies.append(copy)
-    for c in range(chunks):
-        a_copies[c, 1].wait_recv()
+            own.start()
+            own_copies.append(own)
+    forward(heads - 1)
+
+    for h in range(heads):
+        for c in range(chunks):
+            a_copies[h, c, 1].wait_recv()
     for copy in f_copies:
         copy.wait()
     for copy in a_copies.values():
         copy.wait_send()
     for copy in w_copies:
         copy.wait()
-    for copy in k_copies + v_copies:
-        copy.wait_send()
+    for copies in k_copies + v_copies:
+        for copy in copies:
+            copy.wait_send()
     for copy in own_copies:
         copy.wait()
 
@@ -287,8 +298,9 @@
         weight = out_weight.reshape(width, groups, feats).transpose(1, 0, 2)
     blocked = (local_blocks, BLOCK, width)
     bf16 = jnp.bfloat16
+    landing = pltpu.VMEM((peers, UNIQ_CAP, BLOCK, head), bf16)
     dma = pltpu.SemaphoreType.DMA
-    any_spec = pl.BlockSpec(memory_space=pl.ANY)
+    any_spec = pl.BlockSpec(memory_space=pltpu.HBM)
     gathered, weights = pl.pallas_call(
         functools.partial(layer_kernel, peers, groups, heads, sliced),
         out_shape=(
@@ -310,29 +322,29 @@
             pltpu.VMEM(blocked, bf16),
             pltpu.VMEM((peers, 8, 128), jnp.int32),
             pltpu.SMEM((peers, 8, 128), jnp.int32),
-            pltpu.VMEM((peers, UNIQ_CAP, BLOCK, width), bf16),
-            pltpu.VMEM((peers, UNIQ_CAP, BLOCK, width), bf16),
-            pltpu.VMEM((peers, UNIQ_CAP, BLOCK, width), bf16),
-            pltpu.VMEM((peers, UNIQ_CAP, BLOCK, width), bf16),
-            pltpu.VMEM((tok // BLOCK, heads, BLOCK, TOPK * BLOCK), bf16),
+            pltpu.VMEM((heads, peers, UNIQ_CAP, BLOCK, head), bf16),
+            pltpu.VMEM((heads, peers, UNIQ_CAP, BLOCK, head), bf16),
+            tuple(landing for _ in range(heads)),
+            tuple(landing for _ in range(heads)),
+            pltpu.VMEM((tok // BLOCK, BLOCK, TOPK * BLOCK), bf16),
+            pltpu.VMEM((tok, head), jnp.float32),
             pltpu.VMEM((tok, width), jnp.float32),
-            pltpu.VMEM((tok, width), jnp.float32),
-            pltpu.VMEM((tok, width), bf16),
+            pltpu.VMEM((heads, tok, head), bf16),
             dma((5,)),
             dma(()),
-            dma((2 + chunks,)),
+            dma((2 + heads * chunks,)),
             dma((peers,)),
             dma((peers,)),
-            dma((peers,)),
-            dma((peers,)),
-            dma((peers,)),
-            dma((peers,)),
+            dma((heads, peers)),
+            dma((heads, peers)),
+            dma((heads, peers)),
+            dma((heads, peers)),
             dma((groups,)),
             dma((groups,)),
-            dma((chunks, groups)),
-            dma((chunks, groups)),
-            dma((chunks, groups)),
-            dma((chunks, groups)),
+            dma((heads, chunks, groups)),
+            dma((heads, chunks, groups)),
+            dma((heads, chunks, groups)),
+            dma((heads, chunks, groups)),
         ],
         compiler_params=pltpu.CompilerParams(
             collective_id=0, has_side_effects=True, vmem_limit_bytes=52 * 2**20

time: 133 us -> 128 us (0.962)
  Pallas kernels: 118 us -> 113 us
    pallas_call x1, Pallas kernels: 118 us -> 113 us  [shards(): pl.pallas_call(functools.partial(layer_kernel, peers, groups, heads, slic...]
where the time goes in v2:
time: 128 us
  Pallas kernels  113 us (88%)
  matrix products  8.58 us (7%)
  local copies, waits for them, and re-layouts  4.04 us (3%)
  other arithmetic  2.19 us (2%)
    pallas_call x1, Pallas kernels, shards(): pl.pallas_call(functools.partial(layer_kernel, peers, groups, heads, slic...  113 us
    dot_general x1, matrix products, shards(): lax.dot_general(weights, gathered, (((0,), (1,)), ((), ())), preferred_el...  8.58 us
    unnamed x7, local copies, waits for them, and re-layouts  3.88 us

profile of v2, /device:TPU:17, one launch (start us, length us, event | category | flops | bytes accessed | tf_op | source)
XLA Modules:
  0.0 128.0 jit_solution(7526439959395674604)
XLA Ops:
  0.0 0.7 add_divide_fusion
  0.7 0.1 broadcast_in_dim.70
  0.7 0.8 copy.12
  1.5 0.1 eq.86
  1.6 0.8 select_reduce_fusion.2
  2.4 0.2 select_reduce_fusion.1
  2.7 0.2 convert_reduce_fusion
  2.8 0.1 iota_compare_fusion
  2.9 0.1 iota_compare_fusion.1
  3.0 0.1 select_reduce_fusion
  3.2 0.0 copy-start
  3.2 1.0 copy-done
  4.2 0.0 copy-start.1
  4.2 1.0 copy-done.1
  5.2 0.0 copy-start.2
  5.3 1.0 copy-done.2
  6.3 113.1 %memory_layer.1 = (bf16[1024,1024]{1,0:T(8,128)(2,1)}, bf16[1024,1792]{1,0:T(8,128)(2,1)}) custom-call(s32[2,32]{1,0:T(2,128)S(1)} %pad_add_fusion.place_ref, s32[8,8,128]{2,1,0:T(8,128)S(1)} %broadcast_in_dim.69.req_ref, f32[1,256]{1,0:T(1,128)S(1)} %bitcast.14, bf16[1024,256]{1,0:T(8,128)(2,1)S(1)} %copy-done, bf16[1024,256]{1,0:T(8,128)(2,1)S(1)} %copy-done.1, ...), custom_call_target="tpu_custom_call" | custom-call | tf_op jit(solution)/shard_map/memory_layer/pallas_call | solution.py:304
  119.4 8.6 %convolution_convert_fusion = bf16[1792,1024]{1,0:T(8,128)(2,1)} fusion(bf16[1024,1792]{1,0:T(8,128)(2,1)} %get-tuple-element.7, bf16[1024,1024]{1,0:T(8,128)(2,1)} %get-tuple-element.8), kind=kOutput, calls=%fused_computation | convolution fusion | flops 3759931392 | bytes 9437184 | tf_op jit(solution)/shard_map/dot_general | solution.py:357
  (5 shorter events, 0.0 us)
Async XLA Ops:
  3.2 1.0 copy-start
  4.2 1.0 copy-start.1
  5.2 1.0 copy-start.2

commit v3 on v2

--- a/solution.py
+++ b/solution.py
@@ -29,11 +29,11 @@
 def layer_kernel(
     peers, groups, heads, sliced,
     place_ref, req_ref, gate_ref, q_hbm, k_hbm, v_hbm, mk_hbm, mv_hbm, w_hbm,
-    ag_hbm, wg_hbm,
+    ag_hbm, wg_hbm, part_hbm,
     q_vm, k_vm, v_vm, mk_vm, mv_vm, req_in, req_sm, send_k, send_v, recv_k, recv_v,
-    probs, coef, local, att,
-    in_sem, smem_sem, own_sem, req_ss, req_rs, k_ss, k_rs, v_ss, v_rs, w_ss, w_rs,
-    a_ss, a_rs, f_ss, f_rs,
+    probs, coef, local, att, ag_vm, wg_vm, part_vm,
+    in_sem, smem_sem, own_sem, own_w_sem, req_ss, req_rs, k_ss, k_rs, v_ss, v_rs, w_ss, w_rs,
+    a_ss, a_rs, f_ss, f_rs, part_sem,
 ):
     me = lax.axis_index("dp")
     tme = lax.axis_index("tensor")
@@ -74,27 +74,34 @@
         copy.start()
         req_copies.append(copy)
 
-    def weight_part(t):
+    def weight_part(t, h):
+        rows = pl.ds(h * head, head)
         if sliced:
-            return w_hbm.at[:, pl.ds(pl.multiple_of(t * feats, 128), feats)]
-        return w_hbm.at[t]
-
-    def weight_place(t):
-        return wg_hbm.at[pl.ds(pl.multiple_of(t * width, 128), width)]
-
-    w_copies = []
-    for m in range(1, groups):
-        peer = flipped(tme, m)
-        copy = pltpu.make_async_remote_copy(
-            src_ref=weight_part(peer), dst_ref=weight_place(tme), send_sem=w_ss.at[m],
-            recv_sem=w_rs.at[m], device_id={"tensor": peer}, device_id_type=MESH,
-        )
-        copy.start()
-        w_copies.append(copy)
-    own_w = pltpu.make_async_copy(weight_part(tme), weight_place(tme), own_sem.at[0])
-    own_w.start()
-
-    own_req = pltpu.make_async_copy(req_ref.at[me], req_in.at[0], own_sem.at[1])
+            return w_hbm.at[rows, pl.ds(pl.multiple_of(t * feats, 128), feats)]
+        return w_hbm.at[t, rows]
+
+    def weight_place(t, h):
+        if h < heads - 1:
+            column = pl.multiple_of(h * groups * head + t * head, 128)
+            return wg_vm.at[pl.ds(column, head)]
+        return wg_hbm.at[pl.ds(pl.multiple_of(t * head, 128), head)]
+
+    w_copies, own_w = [], []
+    for h in range(heads):
+        for m in range(1, groups):
+            peer = flipped(tme, m)
+            copy = pltpu.make_async_remote_copy(
+                src_ref=weight_part(peer, h), dst_ref=weight_place(tme, h),
+                send_sem=w_ss.at[h, m], recv_sem=w_rs.at[h, m], device_id={"tensor": peer},
+                device_id_type=MESH,
+            )
+            copy.start()
+            w_copies.append(copy)
+        own = pltpu.make_async_copy(weight_part(tme, h), weight_place(tme, h), own_w_sem.at[h])
+        own.start()
+        own_w.append(own)
+
+    own_req = pltpu.make_async_copy(req_ref.at[me], req_in.at[0], own_sem.at[0])
     own_req.start()
     own_req.wait()
     for copy in req_copies:
@@ -121,12 +128,27 @@
             recv[h][me, c] = source[req_sm[0, 0, c], :, cols]
         return copies
 
-    k_copies, v_copies = [], []
-    for h in range(heads):
-        k_copies.append(ship(mk_vm, h, send_k, recv_k, k_ss, k_rs))
-        if h == 0:
-            loads[1].wait()
-        v_copies.append(ship(mv_vm, h, send_v, recv_v, v_ss, v_rs))
+    shipped = []
+
+    def ship_next():
+        stage = len(shipped)
+        h = stage // 2
+        if stage % 2 == 0:
+            shipped.append(ship(mk_vm, h, send_k, recv_k, k_ss, k_rs))
+        else:
+            shipped.append(ship(mv_vm, h, send_v, recv_v, v_ss, v_rs))
+
+    def follow(stage):
+        for copy in shipped[stage]:
+            copy.wait_send()
+        if len(shipped) < 2 * heads:
+            ship_next()
+        for copy in shipped[stage]:
+            copy.wait_recv()
+
+    ship_next()
+    loads[1].wait()
+    ship_next()
     for load in loads[2:]:
         load.wait()
 
@@ -189,13 +211,15 @@
         return carry
 
     def att_place(t, h, c):
-        column = pl.multiple_of(t * width + h * head, 128)
+        column = pl.multiple_of(t * head, 128)
+        if h < heads - 1:
+            column = pl.multiple_of(h * groups * head + t * head, 128)
+            return ag_vm.at[pl.ds(c * crow, crow), pl.ds(column, head)]
         return ag_hbm.at[pl.ds(c * crow, crow), pl.ds(column, head)]
 
     mate = flipped(tme, 1)
     others = list(range(2, groups, 2))
-    a_copies, f_copies = {}, []
-    own_copies = [own_w]
+    a_copies, f_copies, own_copies = {}, {}, {}
 
     def forward(h):
         for c in range(chunks):
@@ -207,16 +231,42 @@
                     recv_sem=f_rs.at[h, c, m], device_id={"tensor": mate}, device_id_type=MESH,
                 )
                 copy.start()
-                f_copies.append(copy)
+                f_copies[h, c, m] = copy
+
+    def settle(h):
+        for c in range(chunks):
+            a_copies[h, c, 1].wait_recv()
+            for m in others:
+                f_copies[h, c, m].wait()
+            for m in others + [1]:
+                a_copies[h, c, m].wait_send()
+            own_copies[h, c].wait()
+
+    tile = 256 if feats % 256 == 0 else feats
+
+    def project(i, carry):
+        at = pl.ds(pl.multiple_of(i * tile, tile), tile) if tile < feats else slice(None)
+        out = lax.dot_general(
+            wg_vm[:, at], ag_vm[...], (((0,), (1,)), ((), ())),
+            preferred_element_type=jnp.float32,
+        )
+        part_vm[at, :] = out.astype(part_vm.dtype)
+        return carry
 
     for h in range(heads):
-        for copy in k_copies[h]:
-            copy.wait_recv()
+        follow(2 * h)
         lax.fori_loop(0, tok // BLOCK, functools.partial(mem_scores, h), 0)
         if h > 0:
             forward(h - 1)
-        for copy in v_copies[h]:
-            copy.wait_recv()
+        if h == heads - 1:
+            for early in range(heads - 1):
+                settle(early)
+            for copy in w_copies + own_w:
+                copy.wait()
+            lax.fori_loop(0, feats // tile, project, 0)
+            part_copy = pltpu.make_async_copy(part_vm, part_hbm, part_sem)
+            part_copy.start()
+        follow(2 * h + 1)
         for c in range(chunks):
             lax.fori_loop(
                 c * crow // BLOCK, (c + 1) * crow // BLOCK, functools.partial(mem_values, h), 0
@@ -231,26 +281,13 @@
                 copy.start()
                 a_copies[h, c, m] = copy
             own = pltpu.make_async_copy(
-                mine, att_place(tme, h, c), own_sem.at[2 + h * chunks + c]
+                mine, att_place(tme, h, c), own_sem.at[1 + h * chunks + c]
             )
             own.start()
-            own_copies.append(own)
+            own_copies[h, c] = own
     forward(heads - 1)
-
-    for h in range(heads):
-        for c in range(chunks):
-            a_copies[h, c, 1].wait_recv()
-    for copy in f_copies:
-        copy.wait()
-    for copy in a_copies.values():
-        copy.wait_send()
-    for copy in w_copies:
-        copy.wait()
-    for copies in k_copies + v_copies:
-        for copy in copies:
-            copy.wait_send()
-    for copy in own_copies:
-        copy.wait()
+    settle(heads - 1)
+    part_copy.wait()
 
 
 def request_plan(retrieved, block_slot, local_blocks, peer_count):
@@ -298,14 +335,16 @@
         weight = out_weight.reshape(width, groups, feats).transpose(1, 0, 2)
     blocked = (local_blocks, BLOCK, width)
     bf16 = jnp.bfloat16
+    early = (heads - 1) * groups * head
     landing = pltpu.VMEM((peers, UNIQ_CAP, BLOCK, head), bf16)
     dma = pltpu.SemaphoreType.DMA
     any_spec = pl.BlockSpec(memory_space=pltpu.HBM)
-    gathered, weights = pl.pallas_call(
+    gathered, weights, partial = pl.pallas_call(
         functools.partial(layer_kernel, peers, groups, heads, sliced),
         out_shape=(
-            jax.ShapeDtypeStruct((tok, groups * width), bf16),
-            jax.ShapeDtypeStruct((groups * width, feats), bf16),
+            jax.ShapeDtypeStruct((tok, groups * head), bf16),
+            jax.ShapeDtypeStruct((groups * head, feats), bf16),
+            jax.ShapeDtypeStruct((feats, tok), bf16),
         ),
         in_specs=[
             pl.BlockSpec(memory_space=pltpu.SMEM),
@@ -313,7 +352,7 @@
             pl.BlockSpec(memory_space=pltpu.VMEM),
         ]
         + [any_spec] * 6,
-        out_specs=(any_spec, any_spec),
+        out_specs=(any_spec, any_spec, any_spec),
         scratch_shapes=[
             pltpu.VMEM((tok, width), bf16),
             pltpu.VMEM((tok, width), bf16),
@@ -330,33 +369,39 @@
             pltpu.VMEM((tok, head), jnp.float32),
             pltpu.VMEM((tok, width), jnp.float32),
             pltpu.VMEM((heads, tok, head), bf16),
+            pltpu.VMEM((tok, early), bf16),
+            pltpu.VMEM((early, feats), bf16),
+            pltpu.VMEM((feats, tok), bf16),
             dma((5,)),
             dma(()),
-            dma((2 + heads * chunks,)),
+            dma((1 + heads * chunks,)),
+            dma((heads,)),
             dma((peers,)),
             dma((peers,)),
             dma((heads, peers)),
             dma((heads, peers)),
             dma((heads, peers)),
             dma((heads, peers)),
-            dma((groups,)),
-            dma((groups,)),
+            dma((heads, groups)),
+            dma((heads, groups)),
             dma((heads, chunks, groups)),
             dma((heads, chunks, groups)),
             dma((heads, chunks, groups)),
             dma((heads, chunks, groups)),
+            dma(()),
         ],
         compiler_params=pltpu.CompilerParams(
-            collective_id=0, has_side_effects=True, vmem_limit_bytes=52 * 2**20
+            collective_id=0, has_side_effects=True, vmem_limit_bytes=62 * 2**20
         ),
         name="memory_layer",
     )(
         place, request, gate_row, queries, keys, values,
         mem_keys.reshape(blocked), mem_values.reshape(blocked), weight,
     )
-    return lax.dot_general(
+    late = lax.dot_general(
         weights, gathered, (((0,), (1,)), ((), ())), preferred_element_type=jnp.float32
-    ).astype(bf16)
+    )
+    return (late + partial.astype(jnp.float32)).astype(bf16)
 
 
 def solution(mesh):

time: 128 us -> 126 us (0.984)
  local copies, waits for them, and re-layouts: 4.04 us -> 2.11 us
  matrix products: 8.58 us -> 6.89 us
    unnamed x7 -> x1, local copies, waits for them, and re-layouts: 3.88 us -> 0.76 us
    dot_general x1, matrix products: 8.58 us -> 6.89 us  [shards(): lax.dot_general(weights, gathered, (((0,), (1,)), ((), ())), preferred_el...]
where the time goes in v3:
time: 126 us; the launch traced here: 125 us
  Pallas kernels  113 us (90%)
  matrix products  6.89 us (5%)
  other arithmetic  2.77 us (2%)
  local copies, waits for them, and re-layouts  2.11 us (2%)
    pallas_call x1, Pallas kernels, shards(): pl.pallas_call(functools.partial(layer_kernel, peers, groups, heads, slic...  113 us
    dot_general x1, matrix products, shards(): lax.dot_general(weights, gathered, (((0,), (1,)), ((), ())), preferred_el...  6.89 us

profile of v3, /device:TPU:17, one launch (start us, length us, event | category | flops | bytes accessed | tf_op | source)
XLA Modules:
  0.0 125.3 jit_solution(6373886477486149533)
XLA Ops:
  0.0 0.7 add_divide_fusion
  0.7 0.7 broadcast_in_dim.70
  1.3 0.8 copy.12
  2.1 0.1 eq.86
  2.2 0.8 select_reduce_fusion.2
  3.0 0.2 select_reduce_fusion.1
  3.2 0.2 convert_reduce_fusion
  3.4 0.6 pad_add_fusion.place_ref
  4.0 0.1 iota_compare_fusion
  4.1 0.1 iota_compare_fusion.1
  4.1 0.1 select_reduce_fusion
  4.3 0.6 broadcast_in_dim.69.req_ref
  4.9 113.5 %memory_layer.1 = (bf16[1024,512]{1,0:T(8,128)(2,1)}, bf16[512,1792]{1,0:T(8,128)(2,1)}, bf16[1792,1024]{1,0:T(8,128)(2,1)}) custom-call(s32[2,32]{1,0:T(2,128)} %pad_add_fusion.place_ref, s32[8,8,128]{2,1,0:T(8,128)} %broadcast_in_dim.69.req_ref, f32[1,256]{1,0:T(1,128)} %bitcast.17, bf16[1024,256]{1,0:T(8,128)(2,1)} %q_hbm.1, bf16[1024,256]{1,0:T(8,128)(2,1)} %k_hbm.1, ...), custom_call_target="tpu_custom_call" | custom-call | tf_op jit(solution)/shard_map/memory_layer/pallas_call | solution.py:342
  118.4 6.9 %add_convert_fusion = bf16[1792,1024]{1,0:T(8,128)(2,1)} fusion(bf16[1792,1024]{1,0:T(8,128)(2,1)} %get-tuple-element.10, bf16[512,1792]{1,0:T(8,128)(2,1)} %get-tuple-element.8, bf16[1024,512]{1,0:T(8,128)(2,1)} %get-tuple-element.9), kind=kOutput, calls=%fused_computation | convolution fusion | flops 1884553216 | bytes 10223616 | tf_op jit(solution)/shard_map/dot_general | solution.py:401
  (3 shorter events, 0.0 us)

commit v4 on v3

--- a/solution.py
+++ b/solution.py
@@ -62,7 +62,7 @@
         )
     pl.semaphore_wait(barrier, peers - 1 + groups - 1)
 
-    order = list(range(peers // 2, peers)) + list(range(peers // 2 - 1, 0, -1))
+    order = list(range(1, peers))
 
     req_copies = []
     for m in order:

time: 126 us -> 124 us (0.984)
  Pallas kernels: 113 us -> 111 us
    pallas_call x1, Pallas kernels: 113 us -> 111 us  [shards(): pl.pallas_call(functools.partial(layer_kernel, peers, groups, heads, slic...]
where the time goes in v4:
time: 124 us; the launch traced here: 122 us
  Pallas kernels  111 us (90%)
  matrix products  6.89 us (6%)
  other arithmetic  2.77 us (2%)
  local copies, waits for them, and re-layouts  2.11 us (2%)
    pallas_call x1, Pallas kernels, shards(): pl.pallas_call(functools.partial(layer_kernel, peers, groups, heads, slic...  111 us
    dot_general x1, matrix products, shards(): lax.dot_general(weights, gathered, (((0,), (1,)), ((), ())), preferred_el...  6.89 us

profile of v4, /device:TPU:17, one launch (start us, length us, event | category | flops | bytes accessed | tf_op | source)
XLA Modules:
  0.0 122.4 jit_solution(17208584306415290498)
XLA Ops:
  0.0 0.7 add_divide_fusion
  0.7 0.7 broadcast_in_dim.70
  1.3 0.8 copy.12
  2.1 0.1 eq.86
  2.2 0.8 select_reduce_fusion.2
  3.0 0.2 select_reduce_fusion.1
  3.2 0.2 convert_reduce_fusion
  3.4 0.6 pad_add_fusion.place_ref
  4.0 0.1 iota_compare_fusion
  4.1 0.1 iota_compare_fusion.1
  4.1 0.1 select_reduce_fusion
  4.3 0.6 broadcast_in_dim.69.req_ref
  4.9 110.6 %memory_layer.1 = (bf16[1024,512]{1,0:T(8,128)(2,1)}, bf16[512,1792]{1,0:T(8,128)(2,1)}, bf16[1792,1024]{1,0:T(8,128)(2,1)}) custom-call(s32[2,32]{1,0:T(2,128)} %pad_add_fusion.place_ref, s32[8,8,128]{2,1,0:T(8,128)} %broadcast_in_dim.69.req_ref, f32[1,256]{1,0:T(1,128)} %bitcast.17, bf16[1024,256]{1,0:T(8,128)(2,1)} %q_hbm.1, bf16[1024,256]{1,0:T(8,128)(2,1)} %k_hbm.1, ...), custom_call_target="tpu_custom_call" | custom-call | tf_op jit(solution)/shard_map/memory_layer/pallas_call | solution.py:342
  115.5 6.9 %add_convert_fusion = bf16[1792,1024]{1,0:T(8,128)(2,1)} fusion(bf16[1792,1024]{1,0:T(8,128)(2,1)} %get-tuple-element.10, bf16[512,1792]{1,0:T(8,128)(2,1)} %get-tuple-element.8, bf16[1024,512]{1,0:T(8,128)(2,1)} %get-tuple-element.9), kind=kOutput, calls=%fused_computation | convolution fusion | flops 1884553216 | bytes 10223616 | tf_op jit(solution)/shard_map/dot_general | solution.py:401
  (3 shorter events, 0.0 us)
